TPU v7x, 32 devices: a whole 2x2x4 slice. The times are simulated.
32 devices in a mesh: tok: 2 (over y), lat: 16 (over z, x, core).
Axes of the slice: x: 2, y: 2, z: 4, core: 2. Of those that a mesh axis runs over, the one named last changes fastest.
Arguments:
- tokens: bfloat16 [512, 8192], P(('tok', 'lat')), may hold values from -6 to 6
- enc_weight: bfloat16 [8192, 4096], P(None, 'lat'), may hold values from -0.0625 to 0.0625
- enc_bias: float32 [4096], P('lat'), may hold values from -3 to 3
- dec_weight: bfloat16 [4096, 8192], P('lat'), may hold values from -0.125 to 0.125
- dec_bias: float32 [8192], replicated, may hold values from -3 to 3
- active_blocks: int32 [4, 8], P('tok'), may hold values from 0 to 15, all different within a row
Outputs:
- reconstruction: bfloat16 [512, 8192], P(('tok', 'lat'))
- enc_grad: float32 [8192, 4096], P('tok', 'lat')
- dec_grad: float32 [4096, 8192], P('lat', 'tok')
Inputs may be any that keep to these rules, and one draw needn't show every extreme that they name: `active_blocks`: each row lists 8 different latent blocks, and every latent block is listed by some row.
All inputs are finite; a program needn't handle non-finite values.
Results may differ from a plain program's by a relative error of at most 0.013.
Values may be sent and summed in bfloat16 or wider, within the bound.
A program may use at most 64 MiB of HBM per device.

v0:
```python
import math

import jax
import jax.numpy as jnp
from jax import lax
from jax.sharding import PartitionSpec as P

LB = 256


def contract_rows(left_rows, right_rows):
    return lax.dot_general(
        left_rows, right_rows, (((0,), (0,)), ((), ())), preferred_element_type=jnp.float32
    )


def shards(tokens, enc_weight, enc_bias, dec_weight, dec_bias, active_blocks):
    tok_dev = tokens.shape[0]
    lat_count = lax.axis_size("lat")
    tok_count = lax.axis_size("tok")
    group_rows = tok_dev * lat_count
    latent_width = enc_weight.shape[1]
    block_count = active_blocks.shape[0]
    block_rows = group_rows // block_count
    blocks_here = latent_width // LB
    owner_index = lax.axis_index("lat")
    cot_scale = 1.0 / math.sqrt(group_rows * tok_count)
    block_ids = owner_index * blocks_here + jnp.arange(blocks_here, dtype=jnp.int32)
    block_hits = jnp.any(active_blocks[:, :, None] == block_ids[None, None, :], axis=1).astype(
        jnp.float32
    )
    latent_gate = jnp.repeat(block_hits, LB, axis=1)[:, None, :]
    bias_row = enc_bias[None, None, :]
    gathered = lax.all_gather(tokens, "lat", axis=0, tiled=True)
    pre_act = (
        jnp.dot(gathered, enc_weight, preferred_element_type=jnp.float32).reshape(
            block_count, block_rows, latent_width
        )
        + bias_row
    )
    activations = (
        (jax.nn.silu(pre_act) * latent_gate).astype(jnp.bfloat16).reshape(group_rows, latent_width)
    )
    bias_dec = dec_bias[None, :]
    partial_sum = jnp.dot(activations, dec_weight, preferred_element_type=jnp.float32)
    decoded_all = lax.psum(partial_sum.astype(jnp.bfloat16), "lat").astype(jnp.float32) + bias_dec
    cot_all = ((decoded_all - gathered.astype(jnp.float32)) * cot_scale).astype(jnp.bfloat16)
    decoded = lax.dynamic_slice_in_dim(decoded_all, owner_index * tok_dev, tok_dev, 0)
    dec_local = contract_rows(activations, cot_all)
    latent_grad = lax.dot_general(
        cot_all, dec_weight, (((1,), (1,)), ((), ())), preferred_element_type=jnp.float32
    )
    sigma = jax.nn.sigmoid(pre_act)
    slope = sigma * (1.0 + pre_act * (1.0 - sigma))
    pre_grad = (
        (latent_grad.reshape(block_count, block_rows, latent_width) * slope * latent_gate)
        .astype(jnp.bfloat16)
        .reshape(group_rows, latent_width)
    )
    enc_local = contract_rows(gathered, pre_grad)
    enc_grad, dec_grad = (
        lax.psum_scatter(
            enc_local.astype(jnp.bfloat16), "tok", scatter_dimension=0, tiled=True
        ).astype(jnp.float32),
        lax.psum_scatter(
            dec_local.astype(jnp.bfloat16), "tok", scatter_dimension=1, tiled=True
        ).astype(jnp.float32),
    )
    return (decoded.astype(jnp.bfloat16), enc_grad, dec_grad)


def solution(mesh):
    placed = (
        P(("tok", "lat"), None),
        P(None, "lat"),
        P("lat"),
        P("lat", None),
        P(),
        P("tok", None),
    )
    return jax.shard_map(
        shards,
        mesh=mesh,
        in_specs=placed,
        out_specs=(P(("tok", "lat"), None), P("tok", "lat"), P("lat", "tok")),
        check_vma=False,
    )
```

profile of v0, /device:TPU:0, one launch (start us, length us, event | category | flops | bytes accessed | tf_op | source)
XLA Modules:
  0.0 310.7 jit_solution(2868739699898427303)
XLA Ops:
  7.2 0.0 all-gather.2.cloned.1.call-start
  7.2 0.7 all-gather.2.cloned.1.call-update
  7.9 0.0 all-reduce.2.cloned.1.call-start
  7.9 0.8 compare_reduce_fusion
  8.8 0.1 broadcast_bitcast_fusion
  8.8 54.4 %all-gather.2.cloned.1.call-done = bf16[256,8192]{1,0:T(8,128)(2,1)} async-done(((bf16[16,8192]{1,0:T(8,128)(2,1)}), bf16[256,8192]{1,0:T(8,128)(2,1)}) %all-gather.2.cloned.1.call-update) | async-done | bytes 4194320 | tf_op jit(solution)/shard_map/all_gather | solution.py:34
  63.3 4.8 %convolution_add_fusion = f32[256,256]{1,0:T(8,128)S(1)} fusion(bf16[256,8192]{1,0:T(8,128)(2,1)} %all-gather.2.cloned.1.call-done, bf16[8192,256]{1,0:T(8,128)(2,1)} %param.7, f32[256]{0:T(256)} %param.8), kind=kOutput, calls=%fused_computation.8 | convolution fusion | flops 1073807360 | bytes 8651776 | tf_op jit(solution)/shard_map/dot_general | solution.py:36
  68.1 0.0 copy-done
  68.1 3.3 %convolution_convert_fusion.2 = bf16[256,8192]{1,0:T(8,128)(2,1)} fusion(bf16[256,8192]{1,0:T(8,128)(2,1)S(1)} %copy-done, f32[256,256]{1,0:T(8,128)S(1)} %convolution_add_fusion, f32[256]{0:T(256)S(1)} %broadcast_bitcast_fusion), kind=kOutput, calls=%fused_computation.2 | convolution fusion | flops 1076232192 | bytes 8651776 | tf_op jit(solution)/shard_map/dot_general | solution.py:45
  71.4 0.0 all-reduce.2.cloned.1.call-update
  71.5 0.0 reduce-scatter.5.cloned.1.call-start
  71.5 109.8 %all-reduce.2.cloned.1.call-done = bf16[256,8192]{1,0:T(8,128)(2,1)} async-done(((bf16[256,8192]{1,0:T(8,128)(2,1)}), bf16[256,8192]{1,0:T(8,128)(2,1)}) %all-reduce.2.cloned.1.call-update) | async-done | bytes 4194320 | tf_op jit(solution)/shard_map/psum | solution.py:46
  181.3 0.0 copy-done.1
  181.3 7.7 %convolution_convert_fusion = bf16[256,8192]{1,0:T(8,128)(2,1)} fusion(bf16[256,8192]{1,0:T(8,128)(2,1)} %all-gather.2.cloned.1.call-done, f32[8192]{0:T(1024)S(1)} %copy-done.1, bf16[256,8192]{1,0:T(8,128)(2,1)} %all-reduce.2.cloned.1.call-done, f32[256,256]{1,0:T(8,128)S(1)} %convolution_add_fusion, f32[256]{0:T(256)S(1)} %broadcast_bitcast_fusion), kind=kOutput, calls=%fused_computation | convolution fusion | flops 1088815104 | bytes 12878848 | tf_op jit(solution)/shard_map/dot_general | solution.py:12
  189.0 0.0 reduce-scatter.5.cloned.1.call-update
  189.0 0.0 reduce-scatter.3.cloned.1.call-start
  189.1 13.1 %fusion = bf16[8192,256]{0,1:T(8,128)(2,1)} fusion(bf16[256,8192]{1,0:T(8,128)(2,1)} %all-gather.2.cloned.1.call-done, bf16[256,8192]{1,0:T(8,128)(2,1)} %param.9, f32[8192]{0:T(1024)S(1)} %copy-done.1, bf16[256,8192]{1,0:T(8,128)(2,1)} %all-reduce.2.cloned.1.call-done, f32[256,256]{1,0:T(8,128)S(1)} %convolution_add_fusion, f32[256]{0:T(256)S(1)} %broadcast_bitcast_fusion), kind=kOutput, calls=%fused_computation.3 | convolution fusion | flops 2162819072 | bytes 17073152 | tf_op jit(solution)/shard_map/dot_general | solution.py:12
  202.2 0.0 reduce-scatter.3.cloned.1.call-update
  202.3 3.6 %convert_add_fusion = bf16[256,8192]{1,0:T(8,128)(2,1)S(1)} fusion(bf16[256,8192]{1,0:T(8,128)(2,1)} %all-reduce.2.cloned.1.call-done, f32[8192]{0:T(1024)S(1)} %copy-done.1), kind=kLoop, calls=%fused_computation.5 | loop fusion | flops 6291456 | bytes 8421376 | tf_op jit(solution)/shard_map/add | solution.py:46
  205.8 0.7 dynamic-slice_convert_fusion
  206.6 36.1 %reduce-scatter.5.cloned.1.call-done = bf16[256,4096]{1,0:T(8,128)(2,1)} async-done(((bf16[256,8192]{1,0:T(8,128)(2,1)}), bf16[256,4096]{1,0:T(8,128)(2,1)}) %reduce-scatter.5.cloned.1.call-update) | async-done | bytes 2097168 | tf_op jit(solution)/shard_map/reduce_scatter | solution.py:65
  242.7 4.1 %convert_element_type.56 = f32[256,4096]{1,0:T(8,128)} convert(bf16[256,4096]{1,0:T(8,128)(2,1)} %reduce-scatter.5.cloned.1.call-done) | non-fusion elementwise | flops 1048576 | bytes 6291456 | tf_op jit(solution)/shard_map/convert_element_type | solution.py:67
  246.8 53.0 %reduce-scatter.3.cloned.1.call-done = bf16[4096,256]{0,1:T(8,128)(2,1)} async-done(((bf16[8192,256]{0,1:T(8,128)(2,1)}), bf16[4096,256]{0,1:T(8,128)(2,1)}) %reduce-scatter.3.cloned.1.call-update) | async-done | bytes 2097168 | tf_op jit(solution)/shard_map/reduce_scatter | solution.py:62
  299.9 4.3 %copy.9 = f32[4096,256]{1,0:T(8,128)} copy(bf16[4096,256]{0,1:T(8,128)(2,1)} %reduce-scatter.3.cloned.1.call-done) | data formatting | bytes 6291456
  (3 shorter events, 0.0 us)
Async XLA Ops:
  7.2 56.1 %all-gather.2.cloned.1.call-start = ((), (), s32[]{:S(2)}) async-start(), calls=%async_computation.2 | async-start | bytes 4456448 | tf_op jit(solution)/shard_map/all_gather | solution.py:34
  7.9 173.4 %all-reduce.2.cloned.1.call-start = ((), (), s32[]{:S(2)}) async-start(), calls=%async_computation.3 | async-start | bytes 8388608 | tf_op jit(solution)/shard_map/psum | solution.py:46
  63.3 4.9 %copy-start = (bf16[256,8192]{1,0:T(8,128)(2,1)S(1)}, bf16[256,8192]{1,0:T(8,128)(2,1)}, u32[]{:S(2)}) copy-start(bf16[256,8192]{1,0:T(8,128)(2,1)} %param.9) | copy-start | bytes 12582916
  71.4 109.9 %copy-start.1 = (f32[8192]{0:T(1024)S(1)}, f32[8192]{0:T(1024)}, u32[]{:S(2)}) copy-start(f32[8192]{0:T(1024)} %param.10) | copy-start | bytes 98308
  71.5 171.3 %reduce-scatter.5.cloned.1.call-start = ((), (), s32[]{:S(2)}) async-start(), calls=%async_computation.5 | async-start | bytes 6291456 | tf_op jit(solution)/shard_map/reduce_scatter | solution.py:65
  189.0 110.8 %reduce-scatter.3.cloned.1.call-start = ((), (), s32[]{:S(2)}) async-start(), calls=%async_computation.4 | async-start | bytes 6291456 | tf_op jit(solution)/shard_map/reduce_scatter | solution.py:62
Sparse Core Ops, SparseCore 0:
  10.1 53.0 all-gather.1
  71.6 109.6 all-reduce.1
  189.2 53.5 reduce-scatter.4
  245.4 54.3 reduce-scatter.2
where the time goes:
time: 311 us
  waiting for transfers between devices  254 us (82%)
  matrix products  29 us (9%)
  between operations  13.8 us (4%)
  other arithmetic  8.47 us (3%)
  local copies, waits for them, and re-layouts  5.09 us (2%)
    psum x1, waiting for transfers between devices, shards(): lax.psum(partial_sum.astype(jnp.bfloat16), 'lat').astype(jnp.float32)  110 us
    all_gather x1, waiting for transfers between devices, shards(): gathered = lax.all_gather(tokens, 'lat', axis=0, tiled=True)  54.4 us
    reduce_scatter x1, waiting for transfers between devices, shards(): lax.psum_scatter(enc_local.astype(jnp.bfloat16), 'tok', scatter_dimension...  53 us
    reduce_scatter x1, waiting for transfers between devices, shards(): lax.psum_scatter(dec_local.astype(jnp.bfloat16), 'tok', scatter_dimension...  36.1 us
    dot_general x2, matrix products, contract_rows(): lax.dot_general(left_rows, right_rows, (((0,), (0,)), ((), ())), preferre...  20.9 us
  transfers between devices with their start and end apart: 4, of which 4 were waited for; matrix products, arithmetic and copies ran while one was open for 7% of the time, Pallas kernels for 0%

commit v1 on v0

--- a/solution.py
+++ b/solution.py
@@ -1,17 +1,350 @@
+import functools
 import math
 
 import jax
 import jax.numpy as jnp
 from jax import lax
+from jax.experimental import pallas as pl
+from jax.experimental.pallas import tpu as pltpu
 from jax.sharding import PartitionSpec as P
 
 LB = 256
+MESH = pl.DeviceIdType.MESH
+NZ, NX, NC = 4, 2, 2
+Z_ORDER = (2, 1, 3)
+BF16 = jnp.bfloat16
+F32 = jnp.float32
 
 
 def contract_rows(left_rows, right_rows):
     return lax.dot_general(
         left_rows, right_rows, (((0,), (0,)), ((), ())), preferred_element_type=jnp.float32
     )
+
+
+def fused_kernel(
+    cot_scale,
+    tok_hbm, encw_hbm, encb_ref, decw_hbm, decb_ref, blocks_ref,
+    recon_ref, toks_out, cots_out, acts_out, grads_out,
+    encw, decw, G, O, C, CO, PT, CR, XS, XR, ZS, ZR, pre, act, act_o, pg, pg_o,
+    local_sem, g_send, g_recv, o_recv, c_send, c_recv, co_recv,
+    r_send, cr_recv, xr_recv, zr_recv, small_send, small_recv,
+):
+    t = lax.axis_index("tok")
+    l = lax.axis_index("lat")
+    z, x, c = l // (NX * NC), (l // NC) % NX, l % NC
+    rows, width = tok_hbm.shape
+    half = width // 2
+
+    def lat_of(dz, dx, dc):
+        zz = lax.rem(z + dz, NZ)
+        xx = x if dx == 0 else 1 - x
+        cc = c if dc == 0 else 1 - c
+        return (zz * NX + xx) * NC + cc
+
+    own = lat_of(0, 0, 0)
+    z_peer = {dz: (t, lat_of(dz, 0, 0)) for dz in Z_ORDER}
+    x_peer = (t, lat_of(0, 1, 0))
+    c_peer = (t, lat_of(0, 0, 1))
+    y_peer = (1 - t, l)
+
+    local = [
+        pltpu.make_async_copy(tok_hbm, G.at[own], local_sem.at[0]),
+        pltpu.make_async_copy(encw_hbm, encw, local_sem.at[1]),
+        pltpu.make_async_copy(decw_hbm, decw, local_sem.at[2]),
+    ]
+    for copy in local:
+        copy.start()
+
+    barrier = pltpu.get_barrier_semaphore()
+    peers = [z_peer[dz] for dz in Z_ORDER] + [x_peer, c_peer, y_peer]
+    for peer in peers:
+        pl.semaphore_signal(barrier, inc=1, device_id=peer, device_id_type=MESH)
+    pl.semaphore_wait(barrier, len(peers))
+
+    sent = []
+
+    def push(src, dst, send_sem, recv_sem, peer):
+        copy = pltpu.make_async_remote_copy(
+            src_ref=src, dst_ref=dst, send_sem=send_sem, recv_sem=recv_sem,
+            device_id=peer, device_id_type=MESH,
+        )
+        copy.start()
+        sent.append(copy)
+
+    def arrived(dst, send_sem, recv_sem):
+        pltpu.make_async_remote_copy(
+            src_ref=dst, dst_ref=dst, send_sem=send_sem, recv_sem=recv_sem,
+            device_id=c_peer, device_id_type=MESH,
+        ).wait_recv()
+
+    mine = pl.ds(pl.multiple_of(t * half, half), half)
+    theirs = pl.ds(pl.multiple_of((1 - t) * half, half), half)
+
+    class Gather:
+        def __init__(self, full, other, send, recv, other_recv):
+            self.full, self.other = full, other
+            self.send, self.recv, self.other_recv = send, recv, other_recv
+            self.count = 0
+
+        def next_send(self):
+            self.count += 1
+            return self.send.at[self.count - 1]
+
+        def give(self, s, peer):
+            push(self.full.at[s], self.full.at[s], self.next_send(), self.recv.at[s], peer)
+
+        def give_y(self, s):
+            push(
+                self.full.at[s, :, theirs], self.other.at[s], self.next_send(),
+                self.other_recv.at[s], y_peer,
+            )
+
+        def take(self, s):
+            arrived(self.full.at[s], self.send.at[0], self.recv.at[s])
+
+        def spread(self):
+            for dz in Z_ORDER:
+                self.give(own, z_peer[dz])
+            self.give(own, x_peer)
+            self.give_y(own)
+            self.give(own, c_peer)
+
+            def from_z(dz):
+                s = lat_of(dz, 0, 0)
+                self.take(s)
+                self.give(s, x_peer)
+                self.give_y(s)
+                self.give(s, c_peer)
+
+            def from_x(dz):
+                s = lat_of(dz, 1, 0)
+                self.take(s)
+                self.give_y(s)
+                self.give(s, c_peer)
+
+            from_z(Z_ORDER[0])
+            from_x(0)
+            for at in range(1, 3):
+                from_z(Z_ORDER[at])
+                from_x(Z_ORDER[at - 1])
+            from_x(Z_ORDER[2])
+
+        def relay_other(self):
+            for dx in range(NX):
+                for dz in (0,) + Z_ORDER:
+                    s = lat_of(dz, dx, 0)
+                    arrived(self.other.at[s], self.send.at[0], self.other_recv.at[s])
+                    push(
+                        self.other.at[s], self.other.at[s], self.next_send(),
+                        self.other_recv.at[s], c_peer,
+                    )
+
+        def settle(self):
+            for dx in range(NX):
+                for dz in (0,) + Z_ORDER:
+                    self.take(lat_of(dz, dx, 1))
+
+        def settle_other(self):
+            for dx in range(NX):
+                for dz in (0,) + Z_ORDER:
+                    s = lat_of(dz, dx, 1)
+                    arrived(self.other.at[s], self.send.at[0], self.other_recv.at[s])
+
+    local[0].wait()
+    toks = Gather(G, O, g_send, g_recv, o_recv)
+    toks.spread()
+    toks.settle()
+
+    group_rows = G.shape[0] * rows
+    lat_width = encw.shape[1]
+    local[1].wait()
+    tile = 1024
+    pre[...] = jnp.broadcast_to(encb_ref[...], pre.shape)
+
+    @pl.loop(0, width // tile)
+    def _(k):
+        cols = pl.ds(pl.multiple_of(k * tile, tile), tile)
+        pre[...] += jnp.dot(
+            G[:, :, cols].reshape(group_rows, tile), encw[cols, :], preferred_element_type=F32
+        )
+
+    block_count = blocks_ref.shape[0]
+    block_rows = group_rows // block_count
+    gates = []
+    for b in range(block_count):
+        hit = blocks_ref[b, 0] == l
+        for slot in range(1, blocks_ref.shape[1]):
+            hit = jnp.logical_or(hit, blocks_ref[b, slot] == l)
+        gates.append(jnp.where(hit, 1.0, 0.0).astype(F32))
+    for b in range(block_count):
+        part = pl.ds(b * block_rows, block_rows)
+        v = pre[part, :]
+        act[part, :] = (v * jax.nn.sigmoid(v) * gates[b]).astype(BF16)
+
+    local[2].wait()
+    tile_d = 512
+
+    @pl.loop(0, width // tile_d)
+    def _(k):
+        cols = pl.ds(pl.multiple_of(k * tile_d, tile_d), tile_d)
+        term = jnp.dot(act[...], decw[:, cols], preferred_element_type=F32)
+        PT[:, :, cols] = term.astype(BF16).reshape(G.shape[0], rows, tile_d)
+
+    at = 0
+    for dx in (1, 0):
+        for dz in Z_ORDER + (0,):
+            s = lat_of(dz, dx, 1)
+            push(PT.at[s], CR.at[s // NC], r_send.at[at], cr_recv.at[s // NC], c_peer)
+            at += 1
+    push(act, act_o, small_send.at[0], small_recv.at[0], y_peer)
+
+    def add_into(dst, *terms):
+        @pl.loop(0, width // tile)
+        def _(k):
+            cols = pl.ds(pl.multiple_of(k * tile, tile), tile)
+            total = terms[0][:, cols].astype(F32)
+            for term in terms[1:]:
+                total = total + term[:, cols].astype(F32)
+            dst[:, cols] = total.astype(BF16)
+
+    for dz in Z_ORDER + (0,):
+        s = lat_of(dz, 1, 0)
+        zz = lax.rem(z + dz, NZ)
+        arrived(CR.at[s // NC], r_send.at[0], cr_recv.at[s // NC])
+        add_into(XS.at[zz], PT.at[s], CR.at[s // NC])
+        push(XS.at[zz], XR.at[zz], r_send.at[at], xr_recv.at[zz], x_peer)
+        at += 1
+    for dz in Z_ORDER:
+        s = lat_of(dz, 0, 0)
+        zz = lax.rem(z + dz, NZ)
+        arrived(CR.at[s // NC], r_send.at[0], cr_recv.at[s // NC])
+        arrived(XR.at[zz], r_send.at[0], xr_recv.at[zz])
+        add_into(ZS.at[zz], PT.at[s], CR.at[s // NC], XR.at[zz])
+        push(ZS.at[zz], ZR.at[z], r_send.at[at], zr_recv.at[z], z_peer[dz])
+        at += 1
+
+    toks.relay_other()
+    toks.settle_other()
+    arrived(act_o, small_send.at[0], small_recv.at[0])
+    out = [
+        pltpu.make_async_copy(G.at[:, :, mine], toks_out.at[0], local_sem.at[3]),
+        pltpu.make_async_copy(O, toks_out.at[1], local_sem.at[4]),
+        pltpu.make_async_copy(act, acts_out.at[0], local_sem.at[5]),
+        pltpu.make_async_copy(act_o, acts_out.at[1], local_sem.at[6]),
+    ]
+    for copy in out:
+        copy.start()
+
+    arrived(CR.at[own // NC], r_send.at[0], cr_recv.at[own // NC])
+    arrived(XR.at[z], r_send.at[0], xr_recv.at[z])
+    for dz in Z_ORDER:
+        zz = lax.rem(z + dz, NZ)
+        arrived(ZR.at[zz], r_send.at[0], zr_recv.at[zz])
+
+    @pl.loop(0, width // tile)
+    def _(k):
+        cols = pl.ds(pl.multiple_of(k * tile, tile), tile)
+        total = PT[own, :, cols].astype(F32) + CR[own // NC, :, cols].astype(F32)
+        total = total + XR[z, :, cols].astype(F32)
+        for dz in Z_ORDER:
+            total = total + ZR[lax.rem(z + dz, NZ), :, cols].astype(F32)
+        total = total + decb_ref[:, cols]
+        recon_ref[:, cols] = total.astype(BF16)
+        C[own, :, cols] = ((total - G[own, :, cols].astype(F32)) * cot_scale).astype(BF16)
+
+    cots = Gather(C, CO, c_send, c_recv, co_recv)
+    cots.spread()
+    cots.relay_other()
+    cots.settle()
+
+    for b in range(block_count):
+        part = pl.ds(b * block_rows, block_rows)
+        v = pre[part, :]
+        sigma = jax.nn.sigmoid(v)
+        pre[part, :] = sigma * (1.0 + v * (1.0 - sigma)) * gates[b]
+    grad = jnp.zeros((group_rows, lat_width), F32)
+
+    def grad_step(k, grad):
+        cols = pl.ds(pl.multiple_of(k * tile, tile), tile)
+        return grad + lax.dot_general(
+            C[:, :, cols].reshape(group_rows, tile), decw[:, cols],
+            (((1,), (1,)), ((), ())), preferred_element_type=F32,
+        )
+
+    grad = lax.fori_loop(0, width // tile, grad_step, grad)
+    pg[...] = (grad * pre[...]).astype(BF16)
+    push(pg, pg_o, small_send.at[1], small_recv.at[1], y_peer)
+    out.append(pltpu.make_async_copy(C.at[:, :, mine], cots_out.at[0], local_sem.at[7]))
+    out[-1].start()
+    cots.settle_other()
+    out.append(pltpu.make_async_copy(CO, cots_out.at[1], local_sem.at[8]))
+    out[-1].start()
+    out.append(pltpu.make_async_copy(pg, grads_out.at[0], local_sem.at[9]))
+    out[-1].start()
+    arrived(pg_o, small_send.at[1], small_recv.at[1])
+    out.append(pltpu.make_async_copy(pg_o, grads_out.at[1], local_sem.at[10]))
+    out[-1].start()
+    for copy in sent:
+        copy.wait_send()
+    for copy in out:
+        copy.wait()
+
+
+def fused_shards(tokens, enc_weight, enc_bias, dec_weight, dec_bias, active_blocks):
+    rows, width = tokens.shape
+    lat_count = lax.axis_size("lat")
+    tok_count = lax.axis_size("tok")
+    group_rows = rows * lat_count
+    latents = enc_weight.shape[1]
+    half = width // tok_count
+    cot_scale = 1.0 / math.sqrt(group_rows * tok_count)
+    hbm = pl.BlockSpec(memory_space=pl.ANY)
+    vmem = pl.BlockSpec(memory_space=pltpu.VMEM)
+    dma = pltpu.SemaphoreType.DMA
+    recon, toks, cots, acts, grads = pl.pallas_call(
+        functools.partial(fused_kernel, cot_scale),
+        out_shape=(
+            jax.ShapeDtypeStruct((rows, width), BF16),
+            jax.ShapeDtypeStruct((2, lat_count, rows, half), BF16),
+            jax.ShapeDtypeStruct((2, lat_count, rows, half), BF16),
+            jax.ShapeDtypeStruct((2, group_rows, latents), BF16),
+            jax.ShapeDtypeStruct((2, group_rows, latents), BF16),
+        ),
+        in_specs=[hbm, hbm, vmem, hbm, vmem, pl.BlockSpec(memory_space=pltpu.SMEM)],
+        out_specs=(vmem, hbm, hbm, hbm, hbm),
+        scratch_shapes=[
+            pltpu.VMEM((width, latents), BF16),
+            pltpu.VMEM((latents, width), BF16),
+            pltpu.VMEM((lat_count, rows, width), BF16),
+            pltpu.VMEM((lat_count, rows, half), BF16),
+            pltpu.VMEM((lat_count, rows, width), BF16),
+            pltpu.VMEM((lat_count, rows, half), BF16),
+            pltpu.VMEM((lat_count, rows, width), BF16),
+            pltpu.VMEM((lat_count // NC, rows, width), BF16),
+            pltpu.VMEM((NZ, rows, width), BF16),
+            pltpu.VMEM((NZ, rows, width), BF16),
+            pltpu.VMEM((NZ, rows, width), BF16),
+            pltpu.VMEM((NZ, rows, width), BF16),
+            pltpu.VMEM((group_rows, latents), F32),
+            pltpu.VMEM((group_rows, latents), BF16),
+            pltpu.VMEM((group_rows, latents), BF16),
+            pltpu.VMEM((group_rows, latents), BF16),
+            pltpu.VMEM((group_rows, latents), BF16),
+            dma((11,)),
+            dma((32,)), dma((16,)), dma((16,)),
+            dma((32,)), dma((16,)), dma((16,)),
+            dma((15,)), dma((8,)), dma((4,)), dma((4,)),
+            dma((2,)), dma((2,)),
+        ],
+        compiler_params=pltpu.CompilerParams(
+            collective_id=0, has_side_effects=True, vmem_limit_bytes=56 * 1024 * 1024
+        ),
+        name="fused_step",
+    )(tokens, enc_weight, enc_bias[None, :], dec_weight, dec_bias[None, :], active_blocks)
+    enc_grad = contract_rows(toks.reshape(2 * group_rows, half), grads.reshape(2 * group_rows, latents))
+    dec_grad = contract_rows(acts.reshape(2 * group_rows, latents), cots.reshape(2 * group_rows, half))
+    return recon, enc_grad, dec_grad
 
 
 def shards(tokens, enc_weight, enc_bias, dec_weight, dec_bias, active_blocks):
@@ -78,8 +411,9 @@
         P(),
         P("tok", None),
     )
+    fits = mesh.shape["tok"] == 2 and mesh.shape["lat"] == NZ * NX * NC
     return jax.shard_map(
-        shards,
+        fused_shards if fits else shards,
         mesh=mesh,
         in_specs=placed,
         out_specs=(P(("tok", "lat"), None), P("tok", "lat"), P("lat", "tok")),

time: 311 us -> 137 us (0.44)
  waiting for transfers between devices: 254 us -> 0 us
  Pallas kernels: 0 us -> 125 us
  matrix products: 29 us -> 8.99 us
  between operations: 13.8 us -> 0.66 us
  other arithmetic: 8.47 us -> 0 us
  local copies, waits for them, and re-layouts: 5.09 us -> 0.71 us
    pallas_call x0 -> x1, Pallas kernels: none -> 125 us  [fused_shards(): pl.pallas_call(functools.partial(fused_kernel, cot_scale), out_shape=(jax...]
    psum x1 -> x0, waiting for transfers between devices: 110 us -> none  [shards(): lax.psum(partial_sum.astype(jnp.bfloat16), 'lat').astype(jnp.float32)]
    reduce_scatter x2 -> x0, waiting for transfers between devices: 89.2 us -> none  [the longest x1 53 us: shards(): lax.psum_scatter(enc_local.astype(jnp.bfloat16), 'tok', scatter_dimension...]
    all_gather x1 -> x0, waiting for transfers between devices: 54.4 us -> none  [shards(): gathered = lax.all_gather(tokens, 'lat', axis=0, tiled=True)]
    dot_general x2, matrix products: 20.9 us -> 8.99 us  [contract_rows(): lax.dot_general(left_rows, right_rows, (((0,), (0,)), ((), ())), preferre...]
    dot_general x2 -> x0, matrix products: 8.16 us -> none  [the longest x1 4.84 us: shards(): jnp.dot(gathered, enc_weight, preferred_element_type=jnp.float32)]
    convert_element_type x2 -> x0, other arithmetic: 4.11 us -> none  [the longest x1 4.1 us: shards(): enc_grad, dec_grad = (lax.psum_scatter(enc_local.astype(jnp.bfloat16), 't...]
    unnamed x5 -> x7, local copies, waits for them, and re-layouts: 4.29 us -> 0.71 us
  transfers between devices with their start and end apart: 4 -> 0, of which waited for: 4 -> 0; matrix products, arithmetic and copies ran while one was open for 7% -> 0% of each run, Pallas kernels for 0% -> 0%
where the time goes in v1:
time: 137 us; the launch traced here: 135 us
  Pallas kernels  125 us (91%)
  matrix products  8.99 us (7%)
    pallas_call x1, Pallas kernels, fused_shards(): pl.pallas_call(functools.partial(fused_kernel, cot_scale), out_shape=(jax...  125 us
    dot_general x2, matrix products, contract_rows(): lax.dot_general(left_rows, right_rows, (((0,), (0,)), ((), ())), preferre...  8.99 us

profile of v1, /device:TPU:0, one launch (start us, length us, event | category | flops | bytes accessed | tf_op | source)
XLA Modules:
  0.0 135.3 jit_solution(14657484459155342302)
XLA Ops:
  0.6 124.9 %fused_step.1 = (bf16[16,8192]{1,0:T(8,128)(2,1)}, bf16[2,16,16,4096]{3,2,1,0:T(8,128)(2,1)}, bf16[2,16,16,4096]{3,2,1,0:T(8,128)(2,1)}, bf16[2,256,256]{2,1,0:T(8,128)(2,1)}, bf16[2,256,256]{2,1,0:T(8,128)(2,1)}) custom-call(bf16[16,8192]{1,0:T(8,128)(2,1)} %tok_hbm.1, bf16[8192,256]{1,0:T(8,128)(2,1)} %encw_hbm.1, f32[1,256]{1,0:T(1,128)} %bitcast.15, ...), custom_call_target="tpu_custom_call" | custom-call | tf_op jit(solution)/shard_map/fused_step/pallas_call | solution.py:305
  125.6 0.0 copy-start
  125.6 0.0 copy-start.1
  125.6 5.7 %fusion = f32[4096,256]{1,0:T(8,128)} fusion(bf16[512,4096]{1,0:T(8,128)(2,1)} %bitcast.11, bf16[512,256]{1,0:T(8,128)(2,1)} %bitcast.13), kind=kOutput, calls=%fused_computation | convolution fusion | flops 1073741824 | bytes 8650752 | tf_op jit(solution)/shard_map/dot_general | solution.py:20
  131.3 0.0 copy-done
  131.3 0.0 copy-done.1
  131.3 0.0 copy-start.2
  131.3 3.3 %fusion.1 = f32[256,4096]{1,0:T(8,128)} fusion(bf16[512,256]{1,0:T(8,128)(2,1)S(1)} %bitcast.12, bf16[512,4096]{1,0:T(8,128)(2,1)S(1)} %bitcast.10), kind=kOutput, calls=%fused_computation.1 | convolution fusion | flops 1073741824 | bytes 8650752 | tf_op jit(solution)/shard_map/dot_general | solution.py:20
  134.6 0.0 copy-done.2
  134.6 0.7 copy.10
Async XLA Ops:
  125.6 5.7 %copy-start = (bf16[2,16,16,4096]{3,2,1,0:T(8,128)(2,1)S(1)}, bf16[2,16,16,4096]{3,2,1,0:T(8,128)(2,1)}, u32[]{:S(2)}) copy-start(bf16[2,16,16,4096]{3,2,1,0:T(8,128)(2,1)} %get-tuple-element.12) | copy-start | bytes 12582916
  125.6 5.7 %copy-start.1 = (bf16[2,256,256]{2,1,0:T(8,128)(2,1)S(1)}, bf16[2,256,256]{2,1,0:T(8,128)(2,1)}, u32[]{:S(2)}) copy-start(bf16[2,256,256]{2,1,0:T(8,128)(2,1)} %get-tuple-element.11) | copy-start | bytes 786436
  131.3 3.3 %copy-start.2 = (bf16[16,8192]{1,0:T(8,128)(2,1)S(1)}, bf16[16,8192]{1,0:T(8,128)(2,1)}, u32[]{:S(2)}) copy-start(bf16[16,8192]{1,0:T(8,128)(2,1)} %get-tuple-element.16) | copy-start | bytes 786436

commit v2 on v1

--- a/solution.py
+++ b/solution.py
@@ -42,7 +42,13 @@
         cc = c if dc == 0 else 1 - c
         return (zz * NX + xx) * NC + cc
 
+    def shard(zz, xx, cc):
+        return (zz * NX + xx) * NC + cc
+
     own = lat_of(0, 0, 0)
+    sources = (z + 1 - 2 * lax.rem(z, 2), 2 - z // 2, 3 - 3 * (z // 2))
+    interior = jnp.logical_and(z >= 1, z <= 2)
+    pair, inner = (t, shard(sources[0], x, c)), (t, shard(3 - z, x, c))
     z_peer = {dz: (t, lat_of(dz, 0, 0)) for dz in Z_ORDER}
     x_peer = (t, lat_of(0, 1, 0))
     c_peer = (t, lat_of(0, 0, 1))
@@ -64,13 +70,16 @@
 
     sent = []
 
-    def push(src, dst, send_sem, recv_sem, peer):
+    def push(src, dst, send_sem, recv_sem, peer, when=None):
         copy = pltpu.make_async_remote_copy(
             src_ref=src, dst_ref=dst, send_sem=send_sem, recv_sem=recv_sem,
             device_id=peer, device_id_type=MESH,
         )
-        copy.start()
-        sent.append(copy)
+        if when is None:
+            copy.start()
+        else:
+            pl.when(when)(lambda: copy.start())
+        sent.append((copy, when))
 
     def arrived(dst, send_sem, recv_sem):
         pltpu.make_async_remote_copy(
@@ -91,8 +100,13 @@
             self.count += 1
             return self.send.at[self.count - 1]
 
-        def give(self, s, peer):
-            push(self.full.at[s], self.full.at[s], self.next_send(), self.recv.at[s], peer)
+        def piece(self, s, h):
+            ref = self.full.at[s, :, theirs if h == 0 else mine]
+            return ref, self.recv.at[s * 2 + h]
+
+        def give(self, peer, s, h, when=None):
+            ref, sem = self.piece(s, h)
+            push(ref, ref, self.next_send(), sem, peer, when)
 
         def give_y(self, s):
             push(
@@ -100,50 +114,63 @@
                 self.other_recv.at[s], y_peer,
             )
 
-        def take(self, s):
-            arrived(self.full.at[s], self.send.at[0], self.recv.at[s])
+        def take(self, s, h):
+            ref, sem = self.piece(s, h)
+            arrived(ref, self.send.at[0], sem)
 
         def spread(self):
-            for dz in Z_ORDER:
-                self.give(own, z_peer[dz])
-            self.give(own, x_peer)
+            self.give(pair, own, 0)
+            self.give(inner, own, 0, interior)
+            self.give(x_peer, own, 0)
             self.give_y(own)
-            self.give(own, c_peer)
-
-            def from_z(dz):
-                s = lat_of(dz, 0, 0)
-                self.take(s)
-                self.give(s, x_peer)
-                self.give_y(s)
-                self.give(s, c_peer)
-
-            def from_x(dz):
-                s = lat_of(dz, 1, 0)
-                self.take(s)
-                self.give_y(s)
-                self.give(s, c_peer)
-
-            from_z(Z_ORDER[0])
-            from_x(0)
-            for at in range(1, 3):
-                from_z(Z_ORDER[at])
-                from_x(Z_ORDER[at - 1])
-            from_x(Z_ORDER[2])
+            self.give(pair, own, 1)
+            self.give(inner, own, 1, interior)
+            self.give(x_peer, own, 1)
+            self.give(c_peer, own, 0)
+            self.give(c_peer, own, 1)
+
+            def from_z(i, h):
+                s = shard(sources[i], x, c)
+                self.take(s, h)
+                self.give(inner if i == 0 else pair, s, h, interior)
+                self.give(x_peer, s, h)
+                if h == 0:
+                    self.give_y(s)
+                self.give(c_peer, s, h)
+
+            def from_x(zz, h):
+                s = shard(zz, 1 - x, c)
+                self.take(s, h)
+                if h == 0:
+                    self.give_y(s)
+                self.give(c_peer, s, h)
+
+            behind = z
+            for i in range(NZ - 1):
+                for h in range(2):
+                    from_z(i, h)
+                    from_x(behind, h)
+                behind = sources[i]
+            for h in range(2):
+                from_x(behind, h)
 
         def relay_other(self):
-            for dx in range(NX):
-                for dz in (0,) + Z_ORDER:
-                    s = lat_of(dz, dx, 0)
-                    arrived(self.other.at[s], self.send.at[0], self.other_recv.at[s])
-                    push(
-                        self.other.at[s], self.other.at[s], self.next_send(),
-                        self.other_recv.at[s], c_peer,
-                    )
+            order = [(z, x), (sources[0], x), (z, 1 - x)]
+            order += [(sources[1], x), (sources[0], 1 - x), (sources[2], x)]
+            order += [(sources[1], 1 - x), (sources[2], 1 - x)]
+            for zz, xx in order:
+                s = shard(zz, xx, c)
+                arrived(self.other.at[s], self.send.at[0], self.other_recv.at[s])
+                push(
+                    self.other.at[s], self.other.at[s], self.next_send(),
+                    self.other_recv.at[s], c_peer,
+                )
 
         def settle(self):
             for dx in range(NX):
                 for dz in (0,) + Z_ORDER:
-                    self.take(lat_of(dz, dx, 1))
+                    for h in range(2):
+                        self.take(lat_of(dz, dx, 1), h)
 
         def settle_other(self):
             for dx in range(NX):
@@ -255,7 +282,6 @@
 
     cots = Gather(C, CO, c_send, c_recv, co_recv)
     cots.spread()
-    cots.relay_other()
     cots.settle()
 
     for b in range(block_count):
@@ -277,6 +303,7 @@
     push(pg, pg_o, small_send.at[1], small_recv.at[1], y_peer)
     out.append(pltpu.make_async_copy(C.at[:, :, mine], cots_out.at[0], local_sem.at[7]))
     out[-1].start()
+    cots.relay_other()
     cots.settle_other()
     out.append(pltpu.make_async_copy(CO, cots_out.at[1], local_sem.at[8]))
     out[-1].start()
@@ -285,8 +312,11 @@
     arrived(pg_o, small_send.at[1], small_recv.at[1])
     out.append(pltpu.make_async_copy(pg_o, grads_out.at[1], local_sem.at[10]))
     out[-1].start()
-    for copy in sent:
-        copy.wait_send()
+    for copy, when in sent:
+        if when is None:
+            copy.wait_send()
+        else:
+            pl.when(when)(lambda: copy.wait_send())
     for copy in out:
         copy.wait()
 
@@ -332,8 +362,8 @@
             pltpu.VMEM((group_rows, latents), BF16),
             pltpu.VMEM((group_rows, latents), BF16),
             dma((11,)),
-            dma((32,)), dma((16,)), dma((16,)),
-            dma((32,)), dma((16,)), dma((16,)),
+            dma((50,)), dma((32,)), dma((16,)),
+            dma((50,)), dma((32,)), dma((16,)),
             dma((15,)), dma((8,)), dma((4,)), dma((4,)),
             dma((2,)), dma((2,)),
         ],

time: 137 us -> 116 us (0.85); the launches traced: 135 us -> 116 us
  Pallas kernels: 125 us -> 105 us
    pallas_call x1, Pallas kernels: 125 us -> 105 us  [fused_shards(): pl.pallas_call(functools.partial(fused_kernel, cot_scale), out_shape=(jax...]
where the time goes in v2:
time: 116 us
  Pallas kernels  105 us (91%)
  matrix products  8.99 us (8%)
    pallas_call x1, Pallas kernels, fused_shards(): pl.pallas_call(functools.partial(fused_kernel, cot_scale), out_shape=(jax...  105 us
    dot_general x2, matrix products, contract_rows(): lax.dot_general(left_rows, right_rows, (((0,), (0,)), ((), ())), preferre...  8.99 us

profile of v2, /device:TPU:0, one launch (start us, length us, event | category | flops | bytes accessed | tf_op | source)
XLA Modules:
  0.0 115.8 jit_solution(13971834493673035800)
XLA Ops:
  0.6 105.4 %fused_step.1 = (bf16[16,8192]{1,0:T(8,128)(2,1)}, bf16[2,16,16,4096]{3,2,1,0:T(8,128)(2,1)}, bf16[2,16,16,4096]{3,2,1,0:T(8,128)(2,1)}, bf16[2,256,256]{2,1,0:T(8,128)(2,1)}, bf16[2,256,256]{2,1,0:T(8,128)(2,1)}) custom-call(bf16[16,8192]{1,0:T(8,128)(2,1)} %tok_hbm.1, bf16[8192,256]{1,0:T(8,128)(2,1)} %encw_hbm.1, f32[1,256]{1,0:T(1,128)} %bitcast.15, ...), custom_call_target="tpu_custom_call" | custom-call | tf_op jit(solution)/shard_map/fused_step/pallas_call | solution.py:335
  106.0 0.0 copy-start
  106.0 0.0 copy-start.1
  106.1 5.7 %fusion = f32[4096,256]{1,0:T(8,128)} fusion(bf16[512,4096]{1,0:T(8,128)(2,1)} %bitcast.11, bf16[512,256]{1,0:T(8,128)(2,1)} %bitcast.13), kind=kOutput, calls=%fused_computation | convolution fusion | flops 1073741824 | bytes 8650752 | tf_op jit(solution)/shard_map/dot_general | solution.py:20
  111.7 0.0 copy-done
  111.7 0.0 copy-done.1
  111.7 0.0 copy-start.2
  111.7 3.3 %fusion.1 = f32[256,4096]{1,0:T(8,128)} fusion(bf16[512,256]{1,0:T(8,128)(2,1)S(1)} %bitcast.12, bf16[512,4096]{1,0:T(8,128)(2,1)S(1)} %bitcast.10), kind=kOutput, calls=%fused_computation.1 | convolution fusion | flops 1073741824 | bytes 8650752 | tf_op jit(solution)/shard_map/dot_general | solution.py:20
  115.1 0.0 copy-done.2
  115.1 0.7 copy.10
Async XLA Ops:
  106.0 5.7 %copy-start = (bf16[2,16,16,4096]{3,2,1,0:T(8,128)(2,1)S(1)}, bf16[2,16,16,4096]{3,2,1,0:T(8,128)(2,1)}, u32[]{:S(2)}) copy-start(bf16[2,16,16,4096]{3,2,1,0:T(8,128)(2,1)} %get-tuple-element.12) | copy-start | bytes 12582916
  106.0 5.7 %copy-start.1 = (bf16[2,256,256]{2,1,0:T(8,128)(2,1)S(1)}, bf16[2,256,256]{2,1,0:T(8,128)(2,1)}, u32[]{:S(2)}) copy-start(bf16[2,256,256]{2,1,0:T(8,128)(2,1)} %get-tuple-element.11) | copy-start | bytes 786436
  111.7 3.3 %copy-start.2 = (bf16[16,8192]{1,0:T(8,128)(2,1)S(1)}, bf16[16,8192]{1,0:T(8,128)(2,1)}, u32[]{:S(2)}) copy-start(bf16[16,8192]{1,0:T(8,128)(2,1)} %get-tuple-element.16) | copy-start | bytes 786436

commit v3 on v2

--- a/solution.py
+++ b/solution.py
@@ -211,23 +211,35 @@
 
     local[2].wait()
     tile_d = 512
-
-    @pl.loop(0, width // tile_d)
-    def _(k):
-        cols = pl.ds(pl.multiple_of(k * tile_d, tile_d), tile_d)
-        term = jnp.dot(act[...], decw[:, cols], preferred_element_type=F32)
-        PT[:, :, cols] = term.astype(BF16).reshape(G.shape[0], rows, tile_d)
-
+    halves = [pl.ds(h * half, half) for h in range(2)]
     at = 0
-    for dx in (1, 0):
+    for h in range(2):
+
+        @pl.loop(h * half // tile_d, (h + 1) * half // tile_d)
+        def _(k):
+            cols = pl.ds(pl.multiple_of(k * tile_d, tile_d), tile_d)
+            term = jnp.dot(act[...], decw[:, cols], preferred_element_type=F32)
+            PT[:, :, cols] = term.astype(BF16).reshape(G.shape[0], rows, tile_d)
+
         for dz in Z_ORDER + (0,):
-            s = lat_of(dz, dx, 1)
-            push(PT.at[s], CR.at[s // NC], r_send.at[at], cr_recv.at[s // NC], c_peer)
+            s = lat_of(dz, 1, 1)
+            push(
+                PT.at[s, :, halves[h]], CR.at[s // NC, :, halves[h]],
+                r_send.at[at], cr_recv.at[s // NC * 2 + h], c_peer,
+            )
+            at += 1
+    for h in range(2):
+        for dz in Z_ORDER + (0,):
+            s = lat_of(dz, 0, 1)
+            push(
+                PT.at[s, :, halves[h]], CR.at[s // NC, :, halves[h]],
+                r_send.at[at], cr_recv.at[s // NC * 2 + h], c_peer,
+            )
             at += 1
     push(act, act_o, small_send.at[0], small_recv.at[0], y_peer)
 
-    def add_into(dst, *terms):
-        @pl.loop(0, width // tile)
+    def add_into(h, dst, *terms):
+        @pl.loop(h * half // tile, (h + 1) * half // tile)
         def _(k):
             cols = pl.ds(pl.multiple_of(k * tile, tile), tile)
             total = terms[0][:, cols].astype(F32)
@@ -235,20 +247,32 @@
                 total = total + term[:, cols].astype(F32)
             dst[:, cols] = total.astype(BF16)
 
-    for dz in Z_ORDER + (0,):
+    def core_in(slot, h):
+        arrived(CR.at[slot, :, halves[h]], r_send.at[0], cr_recv.at[slot * 2 + h])
+
+    def x_in(zz, h):
+        arrived(XR.at[zz, :, halves[h]], r_send.at[0], xr_recv.at[zz * 2 + h])
+
+    for dz, h in [(dz, h) for h in range(2) for dz in Z_ORDER] + [(0, 0), (0, 1)]:
         s = lat_of(dz, 1, 0)
         zz = lax.rem(z + dz, NZ)
-        arrived(CR.at[s // NC], r_send.at[0], cr_recv.at[s // NC])
-        add_into(XS.at[zz], PT.at[s], CR.at[s // NC])
-        push(XS.at[zz], XR.at[zz], r_send.at[at], xr_recv.at[zz], x_peer)
+        core_in(s // NC, h)
+        add_into(h, XS.at[zz], PT.at[s], CR.at[s // NC])
+        push(
+            XS.at[zz, :, halves[h]], XR.at[zz, :, halves[h]],
+            r_send.at[at], xr_recv.at[zz * 2 + h], x_peer,
+        )
         at += 1
-    for dz in Z_ORDER:
+    for dz, h in [(dz, h) for h in range(2) for dz in Z_ORDER]:
         s = lat_of(dz, 0, 0)
         zz = lax.rem(z + dz, NZ)
-        arrived(CR.at[s // NC], r_send.at[0], cr_recv.at[s // NC])
-        arrived(XR.at[zz], r_send.at[0], xr_recv.at[zz])
-        add_into(ZS.at[zz], PT.at[s], CR.at[s // NC], XR.at[zz])
-        push(ZS.at[zz], ZR.at[z], r_send.at[at], zr_recv.at[z], z_peer[dz])
+        core_in(s // NC, h)
+        x_in(zz, h)
+        add_into(h, ZS.at[zz], PT.at[s], CR.at[s // NC], XR.at[zz])
+        push(
+            ZS.at[zz, :, halves[h]], ZR.at[z, :, halves[h]],
+            r_send.at[at], zr_recv.at[z * 2 + h], z_peer[dz],
+        )
         at += 1
 
     toks.relay_other()
@@ -263,11 +287,12 @@
     for copy in out:
         copy.start()
 
-    arrived(CR.at[own // NC], r_send.at[0], cr_recv.at[own // NC])
-    arrived(XR.at[z], r_send.at[0], xr_recv.at[z])
-    for dz in Z_ORDER:
-        zz = lax.rem(z + dz, NZ)
-        arrived(ZR.at[zz], r_send.at[0], zr_recv.at[zz])
+    for h in range(2):
+        core_in(own // NC, h)
+        x_in(z, h)
+        for dz in Z_ORDER:
+            zz = lax.rem(z + dz, NZ)
+            arrived(ZR.at[zz, :, halves[h]], r_send.at[0], zr_recv.at[zz * 2 + h])
 
     @pl.loop(0, width // tile)
     def _(k):
@@ -364,7 +389,7 @@
             dma((11,)),
             dma((50,)), dma((32,)), dma((16,)),
             dma((50,)), dma((32,)), dma((16,)),
-            dma((15,)), dma((8,)), dma((4,)), dma((4,)),
+            dma((30,)), dma((16,)), dma((8,)), dma((8,)),
             dma((2,)), dma((2,)),
         ],
         compiler_params=pltpu.CompilerParams(

time: 116 us -> 113 us (0.974)
  Pallas kernels: 105 us -> 102 us
    pallas_call x1, Pallas kernels: 105 us -> 102 us  [fused_shards(): pl.pallas_call(functools.partial(fused_kernel, cot_scale), out_shape=(jax...]
where the time goes in v3:
time: 113 us
  Pallas kernels  102 us (90%)
  matrix products  8.99 us (8%)
    pallas_call x1, Pallas kernels, fused_shards(): pl.pallas_call(functools.partial(fused_kernel, cot_scale), out_shape=(jax...  102 us
    dot_general x2, matrix products, contract_rows(): lax.dot_general(left_rows, right_rows, (((0,), (0,)), ((), ())), preferre...  8.99 us

profile of v3, /device:TPU:0, one launch (start us, length us, event | category | flops | bytes accessed | tf_op | source)
XLA Modules:
  0.0 112.8 jit_solution(8098403372685295054)
XLA Ops:
  0.6 102.4 %fused_step.1 = (bf16[16,8192]{1,0:T(8,128)(2,1)}, bf16[2,16,16,4096]{3,2,1,0:T(8,128)(2,1)}, bf16[2,16,16,4096]{3,2,1,0:T(8,128)(2,1)}, bf16[2,256,256]{2,1,0:T(8,128)(2,1)}, bf16[2,256,256]{2,1,0:T(8,128)(2,1)}) custom-call(bf16[16,8192]{1,0:T(8,128)(2,1)} %tok_hbm.1, bf16[8192,256]{1,0:T(8,128)(2,1)} %encw_hbm.1, f32[1,256]{1,0:T(1,128)} %bitcast.15, ...), custom_call_target="tpu_custom_call" | custom-call | tf_op jit(solution)/shard_map/fused_step/pallas_call | solution.py:360
  103.1 0.0 copy-start
  103.1 0.0 copy-start.1
  103.1 5.7 %fusion = f32[4096,256]{1,0:T(8,128)} fusion(bf16[512,4096]{1,0:T(8,128)(2,1)} %bitcast.11, bf16[512,256]{1,0:T(8,128)(2,1)} %bitcast.13), kind=kOutput, calls=%fused_computation | convolution fusion | flops 1073741824 | bytes 8650752 | tf_op jit(solution)/shard_map/dot_general | solution.py:20
  108.8 0.0 copy-done
  108.8 0.0 copy-done.1
  108.8 0.0 copy-start.2
  108.8 3.3 %fusion.1 = f32[256,4096]{1,0:T(8,128)} fusion(bf16[512,256]{1,0:T(8,128)(2,1)S(1)} %bitcast.12, bf16[512,4096]{1,0:T(8,128)(2,1)S(1)} %bitcast.10), kind=kOutput, calls=%fused_computation.1 | convolution fusion | flops 1073741824 | bytes 8650752 | tf_op jit(solution)/shard_map/dot_general | solution.py:20
  112.1 0.0 copy-done.2
  112.1 0.7 copy.10
Async XLA Ops:
  103.1 5.7 %copy-start = (bf16[2,16,16,4096]{3,2,1,0:T(8,128)(2,1)S(1)}, bf16[2,16,16,4096]{3,2,1,0:T(8,128)(2,1)}, u32[]{:S(2)}) copy-start(bf16[2,16,16,4096]{3,2,1,0:T(8,128)(2,1)} %get-tuple-element.12) | copy-start | bytes 12582916
  103.1 5.7 %copy-start.1 = (bf16[2,256,256]{2,1,0:T(8,128)(2,1)S(1)}, bf16[2,256,256]{2,1,0:T(8,128)(2,1)}, u32[]{:S(2)}) copy-start(bf16[2,256,256]{2,1,0:T(8,128)(2,1)} %get-tuple-element.11) | copy-start | bytes 786436
  108.8 3.3 %copy-start.2 = (bf16[16,8192]{1,0:T(8,128)(2,1)S(1)}, bf16[16,8192]{1,0:T(8,128)(2,1)}, u32[]{:S(2)}) copy-start(bf16[16,8192]{1,0:T(8,128)(2,1)} %get-tuple-element.16) | copy-start | bytes 786436
